TPU v7x, 256 devices: a whole 4x4x8 slice. The times are simulated.
256 devices in a mesh: dp: 16 (over x, y), seq: 8 (over z_hi, core), mp: 2 (over z_lo).
Axes of the slice: x: 4, y: 4, z: 8 (z_hi: 4, z_lo: 2; z = z_hi * 2 + z_lo), core: 2. Of those that a mesh axis runs over, the one named last changes fastest.
Arguments:
- hidden_states: bfloat16 [8192, 2048], P(('dp', 'seq')), may hold values from -6 to 6
- embeddings: bfloat16 [8192, 2048], P(('dp', 'seq')), may hold values from -6 to 6
- norm_gain: float32 [4096], replicated, may hold values from 0.1 to 1.9
- input_weights: bfloat16 [4096, 3, 2, 2048], P('dp', None, 'mp', 'seq'), may hold values from -0.09375 to 0.09375
- adapter_down: bfloat16 [4096, 384], P(('seq', 'mp')), may hold values from -0.09375 to 0.09375
- adapter_up: bfloat16 [3, 128, 2, 2048], P(None, None, 'mp', 'seq'), may hold values from -0.5 to 0.5
- output_weights: bfloat16 [2, 2048, 2048], P('mp', 'seq', 'dp'), may hold values from -3 to 3
- own_keys: bfloat16 [16, 8192, 4096], P('dp', 'seq', 'mp'), may hold values from -164 to 164
- own_values: bfloat16 [16, 8192, 4096], P('dp', 'seq', 'mp'), may hold values from -6 to 6
- shared_keys: bfloat16 [2, 1024, 4096], P(None, 'seq', 'mp'), may hold values from -164 to 164
- shared_values: bfloat16 [2, 1024, 4096], P(None, 'seq', 'mp'), may hold values from -6 to 6
- cached_lengths: int32 [16], P('dp'), may hold values from 1 to 8192, 65536 in all
- prompt_group: int32 [16], P('dp'), may hold values from 0 to 1
- slot_pages: int32 [16, 128], P('dp', 'seq'), may hold values from 0 to 127, as said below
- padding_mask: int32 [8192], P(('dp', 'seq', 'mp')), may hold values from 0 to 1, as said below
Outputs:
- mixed: bfloat16 [8192, 2048], P(('dp', 'seq', 'mp'))
Inputs may be any that keep to these rules, and one draw needn't show every extreme that they name: `slot_pages`: row r maps the 128 page slots of request r one to one onto its pages: slot u holds page (u + c * 16) mod 128 for a whole number c of request r; page p holds own positions p * 64 to p * 64 + 63. `padding_mask`: within each request's 512 tokens the ones come first, then the zeros; at least 128 ones.
All inputs are finite; a program needn't handle non-finite values. No bound on the sum of `cached_lengths` on one device may be relied on, other than what follows from the above.
Results may differ from a plain program's by a relative error of at most 0.025.
The roundings to bfloat16 on the way count: a program that leaves them out, or rounds other values in their place, can miss the bound.
Values may be sent and summed in bfloat16 or wider, within the bound.
A program may use at most 128 MiB of HBM per device.

v0:
```python
import math
import jax
import jax.numpy as jnp
from jax import lax
from jax.sharding import PartitionSpec as P

HD = 128
PAGE = 64
eps = 1e-05
neg_fill = -1e30
head_block = 4


def joined_2(array, axis, combine):
    everything = jax.tree.map(lambda part: lax.all_gather(part, axis), array)
    leading = jax.tree.map(lambda part: part[0], everything)

    def hop(k, so_far):
        return combine(so_far, jax.tree.map(lambda part: part[k], everything))

    return lax.fori_loop(1, lax.axis_size(axis), hop, leading)


def normalize(hidden_states, embeddings, norm_gain):
    joined = jnp.concatenate([hidden_states, embeddings], axis=1).astype(jnp.float32)
    factor = lax.rsqrt(jnp.mean(joined * joined, axis=1, keepdims=True) + eps)
    return (joined * factor * norm_gain).astype(jnp.bfloat16)


def block_partial(queries, keys, values, usable):
    head_count = queries.shape[1]
    group_size = min(head_block, head_count)
    scaling = 1.0 / math.sqrt(queries.shape[2])

    def one_group(group_index):
        offset = group_index * group_size
        query_part = lax.dynamic_slice_in_dim(queries, offset, group_size, 1)
        key_part = lax.dynamic_slice_in_dim(keys, offset, group_size, 1)
        value_part = lax.dynamic_slice_in_dim(values, offset, group_size, 1)
        scores = (
            jnp.einsum("ihd,jhd->hij", query_part, key_part, preferred_element_type=jnp.float32)
            * scaling
        )
        scores = jnp.where(usable[None], scores, neg_fill)
        peak_score = jnp.max(scores, axis=2)
        exponent = jnp.exp(scores - peak_score[:, :, None])
        totals = jnp.sum(exponent, axis=2)
        weighted = jnp.einsum(
            "hij,jhd->ihd",
            exponent.astype(jnp.bfloat16),
            value_part,
            preferred_element_type=jnp.float32,
        )
        weighted = weighted / jnp.transpose(totals)[:, :, None]
        return (weighted.astype(jnp.bfloat16), jnp.transpose(peak_score), jnp.transpose(totals))

    outputs, peak_rows, total_rows = lax.map(one_group, jnp.arange(head_count // group_size))
    row_count = queries.shape[0]
    outputs = jnp.transpose(outputs, (1, 0, 2, 3)).reshape(row_count, head_count, queries.shape[2])
    peak_rows = jnp.transpose(peak_rows, (1, 0, 2)).reshape(row_count, head_count)
    total_rows = jnp.transpose(total_rows, (1, 0, 2)).reshape(row_count, head_count)
    return (outputs, peak_rows, total_rows)


def join_partials(earlier, later):
    out_first, peak_first, total_first = earlier
    out_second, peak_second, total_second = later
    highest = jnp.maximum(peak_first, peak_second)
    weight_first = total_first * jnp.exp(peak_first - highest)
    weight_second = total_second * jnp.exp(peak_second - highest)
    summed = weight_first + weight_second
    joined = (weight_first[..., None] * out_first + weight_second[..., None] * out_second) / summed[
        ..., None
    ]
    return (joined, highest, summed)


def fold_partials(outputs, peak_scores, totals):
    highest = jnp.max(peak_scores, axis=0)
    weight = totals * jnp.exp(peak_scores - highest)
    return jnp.sum(weight[..., None] * outputs, axis=0) / jnp.sum(weight, axis=0)[..., None]


def shards(
    hidden_states,
    embeddings,
    norm_gain,
    input_weights,
    adapter_down,
    adapter_up,
    output_weights,
    own_keys,
    own_values,
    shared_keys,
    shared_values,
    cached_lengths,
    prompt_group,
    slot_pages,
    padding_mask,
):
    normed = normalize(hidden_states, embeddings, norm_gain)
    gathered = lax.all_gather(normed, "seq", axis=0, tiled=True)
    new_count = gathered.shape[0]
    columns = gathered
    low_sum = jnp.dot(
        columns,
        lax.all_gather(adapter_down, ("seq", "mp"), axis=0, tiled=True),
        preferred_element_type=jnp.float32,
    )
    low_rank = low_sum.astype(jnp.bfloat16)
    width = input_weights.shape[3]
    piece = lax.all_gather(input_weights, "dp", axis=0, tiled=True)
    columns = gathered
    base_terms = jnp.dot(
        columns, piece.reshape(piece.shape[0], 3 * width), preferred_element_type=jnp.float32
    )
    rank_size = adapter_up.shape[1]
    lifted = jnp.einsum(
        "ipr,prc->ipc",
        low_rank.reshape(new_count, 3, rank_size),
        adapter_up[:, :, 0, :],
        preferred_element_type=jnp.float32,
    )
    projected = (base_terms.reshape(new_count, 3, width) + lifted).astype(jnp.bfloat16)
    query_local = projected[:, 0]
    key_local = projected[:, 1]
    value_local = projected[:, 2]
    local_heads = width // HD
    query_all = lax.all_gather(query_local, "seq", axis=1, tiled=True)
    mp_heads = query_all.shape[1] // HD
    group_index = prompt_group[0]
    shared_k = lax.dynamic_index_in_dim(shared_keys, group_index, 0, keepdims=False)
    shared_v = lax.dynamic_index_in_dim(shared_values, group_index, 0, keepdims=False)
    slot_count = own_keys.shape[1]
    cache_keys = jnp.concatenate([own_keys[0], shared_k], axis=0).reshape(-1, mp_heads, HD)
    cache_values = jnp.concatenate([own_values[0], shared_v], axis=0).reshape(-1, mp_heads, HD)
    positions = (
        jnp.repeat(slot_pages[0], PAGE, total_repeat_length=slot_count) * PAGE
        + jnp.arange(slot_count, dtype=jnp.int32) % PAGE
    )
    usable = jnp.concatenate(
        [positions < cached_lengths[0], jnp.ones((shared_k.shape[0],), dtype=jnp.bool_)]
    )[None, :]
    cache_out, cache_peak, cache_total = block_partial(
        query_all.reshape(new_count, mp_heads, HD), cache_keys, cache_values, usable
    )
    places = jnp.arange(new_count, dtype=jnp.int32)
    causal = places[:, None] >= places[None, :]
    new_out, new_peak, new_total = block_partial(
        query_local.reshape(new_count, local_heads, HD),
        key_local.reshape(new_count, local_heads, HD),
        value_local.reshape(new_count, local_heads, HD),
        causal,
    )
    merged_out, merged_peak, merged_total = joined_2(
        (cache_out.astype(jnp.float32), cache_peak, cache_total), "seq", join_partials
    )
    first_head = lax.axis_index("seq") * local_heads
    own_out = lax.dynamic_slice_in_dim(merged_out, first_head, local_heads, 1)
    own_peak = lax.dynamic_slice_in_dim(merged_peak, first_head, local_heads, 1)
    own_total = lax.dynamic_slice_in_dim(merged_total, first_head, local_heads, 1)
    outputs = jnp.stack([own_out, new_out.astype(jnp.float32)])
    peak_scores = jnp.stack([own_peak, new_peak])
    totals = jnp.stack([own_total, new_total])
    attended = (
        fold_partials(outputs, peak_scores, totals)
        .astype(jnp.bfloat16)
        .reshape(new_count, local_heads * HD)
    )
    out_matrix = lax.all_gather(output_weights, "dp", axis=2, tiled=True)[0]
    summed = lax.psum_scatter(
        jnp.dot(attended, out_matrix, preferred_element_type=jnp.float32).astype(jnp.bfloat16),
        ("seq", "mp"),
        scatter_dimension=0,
        tiled=True,
    ).astype(jnp.float32)
    return (padding_mask.astype(jnp.float32)[:, None] * summed).astype(jnp.bfloat16)


def solution(mesh):
    placed = (
        P(("dp", "seq"), None),
        P(("dp", "seq"), None),
        P(),
        P("dp", None, "mp", "seq"),
        P(("seq", "mp"), None),
        P(None, None, "mp", "seq"),
        P("mp", "seq", "dp"),
        P("dp", "seq", "mp"),
        P("dp", "seq", "mp"),
        P(None, "seq", "mp"),
        P(None, "seq", "mp"),
        P("dp"),
        P("dp"),
        P("dp", "seq"),
        P(("dp", "seq", "mp")),
    )
    return jax.shard_map(
        shards, mesh=mesh, in_specs=placed, out_specs=P(("dp", "seq", "mp"), None), check_vma=False
    )
```

profile of v0, /device:TPU:1, one launch (start us, length us, event | category | flops | bytes accessed | tf_op | source)
XLA Modules:
  0.0 744.2 jit_solution(12947220724132167045)
XLA Ops:
  7.3 1.2 fusion.45
  8.6 2.0 fusion.47
  10.7 1.9 copy.54
  12.6 64.0 %all-gather.12.cloned.1.call-done = bf16[4096,384]{1,0:T(8,128)(2,1)} async-done(((bf16[256,384]{1,0:T(8,128)(2,1)}), bf16[4096,384]{1,0:T(8,128)(2,1)}) %all-gather.12.cloned.1.call-update) | async-done | bytes 3145744 | tf_op jit(solution)/shard_map/all_gather | solution.py:107
  76.6 54.6 %all-gather.8.cloned.1.call-done = bf16[512,4096]{1,0:T(8,128)(2,1)} async-done(((bf16[64,4096]{1,0:T(8,128)(2,1)}), bf16[512,4096]{1,0:T(8,128)(2,1)}) %all-gather.8.cloned.1.call-update) | async-done | bytes 4194320 | tf_op jit(solution)/shard_map/all_gather | solution.py:102
  131.2 5.0 convolution_convert_fusion.1
  136.2 65.8 %all-gather.10.cloned.1.call-done = bf16[4096,3,1,256]{0,3,1,2:T(8,128)(2,1)} async-done(((bf16[256,3,1,256]{0,3,1,2:T(8,128)(2,1)}), bf16[4096,3,1,256]{0,3,1,2:T(8,128)(2,1)}) %all-gather.10.cloned.1.call-update) | async-done | bytes 6291472 | tf_op jit(solution)/shard_map/all_gather | solution.py:112
  202.0 6.8 fusion.34
  209.3 0.9 fusion.67
  211.1 2.2 constant_dynamic-slice_fusion.4
  213.5 6.5 copy.52
  220.7 1.3 copy.81
  222.0 6.4 copy.57
  229.3 4.3 compare_select_fusion.1
  233.7 5.6 fusion.58
  239.4 5.1 pad_maximum_fusion
  244.5 2.8 pad_maximum_fusion.1
  247.7 42.9 %while.40 = (s32[]{:T(128)}, bf16[4,512,4,128]{1,3,2,0:T(8,128)(2,1)S(1)}, f32[4,512,4]{1,2,0:T(4,128)S(1)}, f32[4,512,4]{1,2,0:T(4,128)S(1)}, s32[4]{0:T(128)S(...) while((s32[]{:T(128)}, ...), condition=%wide.region_4.5_spmd, body=%wide.region_1.0_spmd.sunk | while | flops 1234432000 | bytes 31798732 | solution.py:57
  248.9 3.2 fusion.85
  252.2 2.3 fusion.86
  254.5 3.9 fusion.87
  259.7 3.2 fusion.85
  262.9 2.3 fusion.86
  265.2 3.9 fusion.87
  270.4 3.2 fusion.85
  273.7 2.3 fusion.86
  275.9 3.9 fusion.87
  281.1 3.2 fusion.85
  284.4 2.3 fusion.86
  286.7 3.9 fusion.87
  290.6 2.5 convert_bitcast_fusion
  293.1 5.5 copy.61
  301.5 18.6 %all_gather.30 = f32[8,512,16]{1,2,0:T(8,128)S(1)} all-gather(f32[1,512,16]{1,2,0:T(8,128)S(1)} %all_gather_reshape.6), channel_id=1, replica_groups=mesh['dp'=16,'seq'=8,'mp'=2] {'seq'}, dimensions={0}, use_global_device_ids=true | all-gather | bytes 294912 | tf_op jit(solution)/shard_map/all_gather | solution.py:15
  320.3 17.8 %all_gather.31 = f32[8,512,16]{1,2,0:T(8,128)S(1)} all-gather(f32[1,512,16]{1,2,0:T(8,128)S(1)} %all_gather_reshape.7), channel_id=1, replica_groups=mesh['dp'=16,'seq'=8,'mp'=2] {'seq'}, dimensions={0}, use_global_device_ids=true | all-gather | bytes 294912 | tf_op jit(solution)/shard_map/all_gather | solution.py:15
  338.2 261.0 %all-gather.14.cloned.1.call-done = f32[8,512,16,128]{3,2,1,0:T(8,128)} async-done(((f32[1,512,16,128]{3,2,1,0:T(8,128)}), f32[8,512,16,128]{3,2,1,0:T(8,128)}) %all-gather.14.cloned.1.call-update) | async-done | bytes 33554448 | tf_op jit(solution)/shard_map/all_gather | solution.py:15
  599.2 4.5 slice_bitcast_fusion
  603.7 66.2 %while.41 = (s32[]{:T(128)}, f32[512,16,128]{2,1,0:T(8,128)}, f32[512,16]{1,0:T(8,128)S(1)}, f32[512,16]{1,0:T(8,128)S(1)}, f32[8,512,16]{1,2,0:T(8,128)S(1)}, /...) while((s32[]{:T(128)}, f32[512,16,128]{2,1,0:T(8,128)}, ...), condition=%wide.region_6.7_spmd, body=%wide.region_5.6_spmd.sunk | while | flops 4243461 | bytes 13205655 | solution.py:21
  604.2 9.0 %fusion.89 = f32[512,16,128]{2,1,0:T(8,128)} fusion(f32[8,512,16,128]{3,2,1,0:T(8,128)} %get-tuple-element.580, s32[]{:T(128)S(6)} %select_n.128, f32[512,16,128]{2,1,0:T(8,128)} %get-tuple-element.565, f32[512,16]{1,0:T(8,128)S(1)} %get-tuple-element.577, f32[512,16]{1,0:T(8,128)S(1)} %get-tuple-element.512, f32[512,16]{1,0:T(8,128)S(1)} %get-tuple-element.513), kind=kLoop, calls=%fused_computation.23.clone.1 | loop fusion | flops 4194304 | bytes 12681220 | tf_op jit(solution)/shard_map/while/body/eval_jaxpr/div | solution.py:72
  613.7 9.0 %fusion.89 = f32[512,16,128]{2,1,0:T(8,128)} fusion(f32[8,512,16,128]{3,2,1,0:T(8,128)} %get-tuple-element.580, s32[]{:T(128)S(6)} %select_n.128, f32[512,16,128]{2,1,0:T(8,128)} %get-tuple-element.565, f32[512,16]{1,0:T(8,128)S(1)} %get-tuple-element.577, f32[512,16]{1,0:T(8,128)S(1)} %get-tuple-element.512, f32[512,16]{1,0:T(8,128)S(1)} %get-tuple-element.513), kind=kLoop, calls=%fused_computation.23.clone.1 | loop fusion | flops 4194304 | bytes 12681220 | tf_op jit(solution)/shard_map/while/body/eval_jaxpr/div | solution.py:72
  623.1 8.9 %fusion.89 = f32[512,16,128]{2,1,0:T(8,128)} fusion(f32[8,512,16,128]{3,2,1,0:T(8,128)} %get-tuple-element.580, s32[]{:T(128)S(6)} %select_n.128, f32[512,16,128]{2,1,0:T(8,128)} %get-tuple-element.565, f32[512,16]{1,0:T(8,128)S(1)} %get-tuple-element.577, f32[512,16]{1,0:T(8,128)S(1)} %get-tuple-element.512, f32[512,16]{1,0:T(8,128)S(1)} %get-tuple-element.513), kind=kLoop, calls=%fused_computation.23.clone.1 | loop fusion | flops 4194304 | bytes 12681220 | tf_op jit(solution)/shard_map/while/body/eval_jaxpr/div | solution.py:72
  632.6 9.0 %fusion.89 = f32[512,16,128]{2,1,0:T(8,128)} fusion(f32[8,512,16,128]{3,2,1,0:T(8,128)} %get-tuple-element.580, s32[]{:T(128)S(6)} %select_n.128, f32[512,16,128]{2,1,0:T(8,128)} %get-tuple-element.565, f32[512,16]{1,0:T(8,128)S(1)} %get-tuple-element.577, f32[512,16]{1,0:T(8,128)S(1)} %get-tuple-element.512, f32[512,16]{1,0:T(8,128)S(1)} %get-tuple-element.513), kind=kLoop, calls=%fused_computation.23.clone.1 | loop fusion | flops 4194304 | bytes 12681220 | tf_op jit(solution)/shard_map/while/body/eval_jaxpr/div | solution.py:72
  642.0 9.0 %fusion.89 = f32[512,16,128]{2,1,0:T(8,128)} fusion(f32[8,512,16,128]{3,2,1,0:T(8,128)} %get-tuple-element.580, s32[]{:T(128)S(6)} %select_n.128, f32[512,16,128]{2,1,0:T(8,128)} %get-tuple-element.565, f32[512,16]{1,0:T(8,128)S(1)} %get-tuple-element.577, f32[512,16]{1,0:T(8,128)S(1)} %get-tuple-element.512, f32[512,16]{1,0:T(8,128)S(1)} %get-tuple-element.513), kind=kLoop, calls=%fused_computation.23.clone.1 | loop fusion | flops 4194304 | bytes 12681220 | tf_op jit(solution)/shard_map/while/body/eval_jaxpr/div | solution.py:72
  651.5 8.9 %fusion.89 = f32[512,16,128]{2,1,0:T(8,128)} fusion(f32[8,512,16,128]{3,2,1,0:T(8,128)} %get-tuple-element.580, s32[]{:T(128)S(6)} %select_n.128, f32[512,16,128]{2,1,0:T(8,128)} %get-tuple-element.565, f32[512,16]{1,0:T(8,128)S(1)} %get-tuple-element.577, f32[512,16]{1,0:T(8,128)S(1)} %get-tuple-element.512, f32[512,16]{1,0:T(8,128)S(1)} %get-tuple-element.513), kind=kLoop, calls=%fused_computation.23.clone.1 | loop fusion | flops 4194304 | bytes 12681220 | tf_op jit(solution)/shard_map/while/body/eval_jaxpr/div | solution.py:72
  660.9 8.9 %fusion.89 = f32[512,16,128]{2,1,0:T(8,128)} fusion(f32[8,512,16,128]{3,2,1,0:T(8,128)} %get-tuple-element.580, s32[]{:T(128)S(6)} %select_n.128, f32[512,16,128]{2,1,0:T(8,128)} %get-tuple-element.565, f32[512,16]{1,0:T(8,128)S(1)} %get-tuple-element.577, f32[512,16]{1,0:T(8,128)S(1)} %get-tuple-element.512, f32[512,16]{1,0:T(8,128)S(1)} %get-tuple-element.513), kind=kLoop, calls=%fused_computation.23.clone.1 | loop fusion | flops 4194304 | bytes 12681220 | tf_op jit(solution)/shard_map/while/body/eval_jaxpr/div | solution.py:72
  669.9 1.8 constant_dynamic-slice_fusion.2
  672.5 3.3 convolution_convert_fusion
  675.9 59.8 %reduce-scatter.2.cloned.1.call-done = bf16[32,2048]{1,0:T(8,128)(2,1)} async-done(((bf16[512,2048]{1,0:T(8,128)(2,1)}), bf16[32,2048]{1,0:T(8,128)(2,1)}) %reduce-scatter.2.cloned.1.call-update) | async-done | bytes 131088 | tf_op jit(solution)/shard_map/reduce_scatter | solution.py:171
  735.7 1.6 multiply_convert_fusion
  (101 shorter events, 13.0 us)
Async XLA Ops:
  6.5 202.3 %copy-start = (bf16[3,128,1,256]{3,1,2,0:T(8,128)(2,1)S(1)}, bf16[3,128,1,256]{3,1,2,0:T(8,128)(2,1)}, u32[]{:S(2)}) copy-start(bf16[3,128,1,256]{3,1,2,0:T(8,128)(2,1)} %param.26) | copy-start | bytes 589828
  6.5 70.1 %all-gather.12.cloned.1.call-start = ((), (), s32[]{:S(2)}) async-start(), calls=%async_computation.3 | async-start | bytes 3342336 | tf_op jit(solution)/shard_map/all_gather | solution.py:107
  7.3 124.0 %all-gather.8.cloned.1.call-start = ((), (), s32[]{:S(2)}) async-start(), calls=%async_computation.1 | async-start | bytes 4718592 | tf_op jit(solution)/shard_map/all_gather | solution.py:102
  10.6 191.4 %all-gather.10.cloned.1.call-start = ((), (), s32[]{:S(2)}) async-start(), calls=%async_computation.2 | async-start | bytes 6684672 | tf_op jit(solution)/shard_map/all_gather | solution.py:112
  12.6 235.1 %all-gather.18.cloned.1.call-start = ((), (), s32[]{:S(2)}) async-start(), calls=%async_computation.7 | async-start | bytes 2359296 | tf_op jit(solution)/shard_map/all_gather | solution.py:129
  210.2 389.0 %all-gather.14.cloned.1.call-start = ((), (), s32[]{:S(2)}) async-start(), calls=%async_computation.4 | async-start | bytes 37748736 | tf_op jit(solution)/shard_map/all_gather | solution.py:15
  222.0 6.5 copy-start.6
  222.0 7.2 copy-start.7
  239.4 5.1 copy-start.2
  298.6 0.9 copy-start.3
  298.6 1.0 copy-start.4
  298.6 2.2 copy-start.5
  298.6 373.9 %all-gather.16.cloned.1.call-start = ((), (), s32[]{:S(2)}) async-start(), calls=%async_computation.5 | async-start | bytes 1114112 | tf_op jit(solution)/shard_map/all_gather | solution.py:170
  299.2 436.5 %reduce-scatter.2.cloned.1.call-start = ((), (), s32[]{:S(2)}) async-start(), calls=%async_computation.6 | async-start | bytes 2228224 | tf_op jit(solution)/shard_map/reduce_scatter | solution.py:171
  672.3 3.6 copy-start.8
  672.3 65.1 %copy-start.1 = (bf16[3,128,1,256]{3,1,2,0:T(8,128)(2,1)S(1)}, bf16[3,128,1,256]{3,1,2,0:T(8,128)(2,1)}, u32[]{:S(2)}) copy-start(bf16[3,128,1,256]{3,1,2,0:T(8,128)(2,1)} %param.26) | copy-start | bytes 589828
Sparse Core Ops, SparseCore 0:
  9.1 67.4 all-gather.11
  78.5 52.7 all-gather.7
  133.7 68.3 all-gather.9
  210.3 37.3 all-gather.17
  298.7 300.4 all-gather.13
  601.5 44.6 all-gather.15
  676.0 59.6 reduce-scatter.1
where the time goes:
time: 747 us; the launch traced here: 744 us
  waiting for transfers between devices  507 us (68%)
  other arithmetic  99.7 us (13%)
  matrix products  45.5 us (6%)
  local copies, waits for them, and re-layouts  37.5 us (5%)
  blocking collectives  36.4 us (5%)
  between operations  15.1 us (2%)
    all_gather x1, waiting for transfers between devices, joined_2(): everything = jax.tree.map(lambda part: lax.all_gather(part, axis), array)  261 us
    all_gather x1, waiting for transfers between devices, shards(): piece = lax.all_gather(input_weights, 'dp', axis=0, tiled=True)  65.8 us
    all_gather x1, waiting for transfers between devices, shards(): lax.all_gather(adapter_down, ('seq', 'mp'), axis=0, tiled=True)  64 us
    div x7, other arithmetic, join_partials(): (weight_first[..., None] * out_first + weight_second[..., None] * out_sec...  62.7 us
    reduce_scatter x1, waiting for transfers between devices, shards(): lax.psum_scatter(jnp.dot(attended, out_matrix, preferred_element_type=jnp...  59.8 us
    all_gather x1, waiting for transfers between devices, shards(): gathered = lax.all_gather(normed, 'seq', axis=0, tiled=True)  54.6 us
    all_gather x2, blocking collectives, joined_2(): everything = jax.tree.map(lambda part: lax.all_gather(part, axis), array)  36.4 us
    unnamed x22, local copies, waits for them, and re-layouts  16.5 us
  transfers between devices with their start and end apart: 7, of which 6 were waited for; matrix products, arithmetic and copies ran while one was open for 16% of the time, Pallas kernels for 0%

commit v1 on v0

--- a/solution.py
+++ b/solution.py
@@ -9,6 +9,25 @@
 eps = 1e-05
 neg_fill = -1e30
 head_block = 4
+
+
+def _drive_gates(row_data, peer_axis):
+    all_values = lax.psum(1, peer_axis)
+    formed = lax.axis_index(peer_axis)
+    w_next, latest, val2 = (all_values, formed, row_data.shape[0])
+    samples = tuple(((i, (i + 1) % w_next) for i in range(w_next)))
+    runs = tuple(((i, (i - 1) % w_next) for i in range(w_next)))
+    z2 = jnp.zeros((*row_data.shape[:0], w_next * val2, *row_data.shape[1:]), row_data.dtype)
+    z2 = lax.dynamic_update_slice_in_dim(z2, row_data, latest * val2, axis=0)
+    t1 = low = row_data
+    after = w_next // 2
+    for src_i in tuple(range(1, after + 1)):
+        t1 = lax.ppermute(t1, peer_axis, samples)
+        z2 = lax.dynamic_update_slice_in_dim(z2, t1, (latest - src_i) % w_next * val2, axis=0)
+        if src_i < w_next - after:
+            low = lax.ppermute(low, peer_axis, runs)
+            z2 = lax.dynamic_update_slice_in_dim(z2, low, (latest + src_i) % w_next * val2, axis=0)
+    return z2
 
 
 def joined_2(array, axis, combine):
@@ -109,7 +128,7 @@
     )
     low_rank = low_sum.astype(jnp.bfloat16)
     width = input_weights.shape[3]
-    piece = lax.all_gather(input_weights, "dp", axis=0, tiled=True)
+    piece = _drive_gates(input_weights, "dp")
     columns = gathered
     base_terms = jnp.dot(
         columns, piece.reshape(piece.shape[0], 3 * width), preferred_element_type=jnp.float32

time: 747 us -> 679 us (0.909)
  waiting for transfers between devices: 507 us -> 390 us
  starting transfers between devices: 0.43 us -> 35.9 us
  local copies, waits for them, and re-layouts: 37.5 us -> 53.5 us
    all_gather x1 -> x0, waiting for transfers between devices: 65.8 us -> none  [shards(): piece = lax.all_gather(input_weights, 'dp', axis=0, tiled=True)]
    all_gather x1, waiting for transfers between devices: 64 us -> 0.01 us  [shards(): lax.all_gather(adapter_down, ('seq', 'mp'), axis=0, tiled=True)]
    ppermute x0 -> x15, waiting for transfers between devices: none -> 36.7 us  [the longest x8 29.3 us: _drive_gates(): t1 = lax.ppermute(t1, peer_axis, samples)]
    ppermute x0 -> x15, starting transfers between devices: none -> 35.5 us  [the longest x7 33.3 us: _drive_gates(): low = lax.ppermute(low, peer_axis, runs)]
    all_gather x1, waiting for transfers between devices: 54.6 us -> 30.3 us  [shards(): gathered = lax.all_gather(normed, 'seq', axis=0, tiled=True)]
    dynamic_update_slice x0 -> x16, local copies, waits for them, and re-layouts: none -> 13.3 us  [the longest x8 6.68 us: _drive_gates(): lax.dynamic_update_slice_in_dim(z2, t1, (latest - src_i) % w_next * val2,...]
    unnamed x22 -> x32, local copies, waits for them, and re-layouts: 16.5 us -> 15.5 us
  transfers between devices with their start and end apart: 7 -> 21, of which waited for: 6 -> 13; matrix products, arithmetic and copies ran while one was open for 16% -> 20% of each run, Pallas kernels for 0% -> 0%
where the time goes in v1:
time: 679 us; the launch traced here: 676 us
  waiting for transfers between devices  390 us (57%)
  other arithmetic  99.8 us (15%)
  local copies, waits for them, and re-layouts  53.5 us (8%)
  matrix products  45 us (7%)
  starting transfers between devices  35.9 us (5%)
  blocking collectives  34.3 us (5%)
  between operations  15.1 us (2%)
    all_gather x1, waiting for transfers between devices, joined_2(): everything = jax.tree.map(lambda part: lax.all_gather(part, axis), array)  261 us
    div x7, other arithmetic, join_partials(): (weight_first[..., None] * out_first + weight_second[..., None] * out_sec...  62.7 us
    reduce_scatter x1, waiting for transfers between devices, shards(): lax.psum_scatter(jnp.dot(attended, out_matrix, preferred_element_type=jnp...  60.9 us
    all_gather x2, blocking collectives, joined_2(): everything = jax.tree.map(lambda part: lax.all_gather(part, axis), array)  34.3 us
    ppermute x7, starting transfers between devices, _drive_gates(): low = lax.ppermute(low, peer_axis, runs)  33.3 us
    all_gather x1, waiting for transfers between devices, shards(): gathered = lax.all_gather(normed, 'seq', axis=0, tiled=True)  30.3 us
    ppermute x8, waiting for transfers between devices, _drive_gates(): t1 = lax.ppermute(t1, peer_axis, samples)  29.3 us
    dot_general x5, matrix products, one_group(): jnp.einsum('hij,jhd->ihd', exponent.astype(jnp.bfloat16), value_part, pre...  16.3 us
  transfers between devices with their start and end apart: 21, of which 13 were waited for; matrix products, arithmetic and copies ran while one was open for 20% of the time, Pallas kernels for 0%

profile of v1, /device:TPU:1, one launch (start us, length us, event | category | flops | bytes accessed | tf_op | source)
XLA Modules:
  0.0 676.4 jit_solution(120031966836470432)
XLA Ops:
  14.0 3.7 collective-permute-start.1
  17.8 6.9 %collective-permute-done = bf16[256,3,1,256]{0,3,1,2:T(8,128)(2,1)S(1)} collective-permute-done((bf16[256,3,1,256]{0,3,1,2:T(8,128)(2,1)S(1)}, bf16[256,3,1,256]{0,3,1,2:T(8,128)(2,1)S(1)}, u32[]{:S(2)}, u32[]{:S(2)}) %collective-permute-start) | collective-permute-done | bytes 393248 | tf_op jit(solution)/shard_map/ppermute | solution.py:25
  24.7 4.8 collective-permute-start.3
  29.4 6.1 collective-permute-done.2
  35.6 4.8 collective-permute-start.5
  40.3 5.2 collective-permute-done.4
  45.5 4.8 collective-permute-start.7
  50.3 5.2 collective-permute-done.6
  55.5 3.4 broadcast_in_dim.96
  60.6 4.8 collective-permute-start.9
  70.1 5.2 collective-permute-start.11
  81.3 5.2 collective-permute-start.13
  90.1 3.6 collective-permute-done.13
  94.5 5.6 collective-permute-done.14
  100.9 30.3 %all-gather.7.cloned.1.call-done = bf16[512,4096]{1,0:T(8,128)(2,1)} async-done(((bf16[64,4096]{1,0:T(8,128)(2,1)}), bf16[512,4096]{1,0:T(8,128)(2,1)}) %all-gather.7.cloned.1.call-update) | async-done | bytes 4194320 | tf_op jit(solution)/shard_map/all_gather | solution.py:121
  131.2 5.1 convolution_convert_fusion.1
  136.8 6.2 fusion.40
  147.3 6.5 copy.54
  155.9 6.4 copy.61
  163.1 4.4 compare_select_fusion.1
  167.7 5.6 fusion.63
  173.3 5.1 pad_maximum_fusion
  178.5 2.8 pad_maximum_fusion.1
  181.3 43.2 %while.40 = (s32[]{:T(128)}, bf16[4,512,4,128]{1,3,2,0:T(8,128)(2,1)S(1)}, f32[4,512,4]{1,2,0:T(4,128)S(1)}, f32[4,512,4]{1,2,0:T(4,128)S(1)}, s32[4]{0:T(128)S(...) while((s32[]{:T(128)}, ...), condition=%wide.region_4.5_spmd, body=%wide.region_1.4_spmd.sunk | while | flops 1234432000 | bytes 31798732 | solution.py:76
  182.6 3.2 fusion.91
  188.2 3.9 fusion.93
  193.4 3.2 fusion.91
  198.9 3.9 fusion.93
  204.2 3.2 fusion.91
  209.7 3.9 fusion.93
  215.0 3.2 fusion.91
  220.5 3.9 fusion.93
  224.5 2.5 convert_bitcast_fusion
  227.0 5.5 copy.65
  235.2 14.8 %all_gather.26 = f32[8,512,16]{1,2,0:T(8,128)S(1)} all-gather(f32[1,512,16]{1,2,0:T(8,128)S(1)} %all_gather_reshape.6), channel_id=1, replica_groups=mesh['dp'=16,'seq'=8,'mp'=2] {'seq'}, dimensions={0}, use_global_device_ids=true | all-gather | bytes 294912 | tf_op jit(solution)/shard_map/all_gather | solution.py:34
  250.2 19.5 %all_gather.27 = f32[8,512,16]{1,2,0:T(8,128)S(1)} all-gather(f32[1,512,16]{1,2,0:T(8,128)S(1)} %all_gather_reshape.7), channel_id=1, replica_groups=mesh['dp'=16,'seq'=8,'mp'=2] {'seq'}, dimensions={0}, use_global_device_ids=true | all-gather | bytes 294912 | tf_op jit(solution)/shard_map/all_gather | solution.py:34
  269.9 260.6 %all-gather.11.cloned.1.call-done = f32[8,512,16,128]{3,2,1,0:T(8,128)} async-done(((f32[1,512,16,128]{3,2,1,0:T(8,128)}), f32[8,512,16,128]{3,2,1,0:T(8,128)}) %all-gather.11.cloned.1.call-update) | async-done | bytes 33554448 | tf_op jit(solution)/shard_map/all_gather | solution.py:34
  530.4 4.5 slice_bitcast_fusion
  534.9 66.1 %while.41 = (s32[]{:T(128)}, f32[512,16,128]{2,1,0:T(8,128)}, f32[512,16]{1,0:T(8,128)S(1)}, f32[512,16]{1,0:T(8,128)S(1)}, f32[8,512,16]{1,2,0:T(8,128)S(1)}, /...) while((s32[]{:T(128)}, f32[512,16,128]{2,1,0:T(8,128)}, ...), condition=%wide.region_6.7_spmd, body=%wide.region_5.6_spmd.sunk | while | flops 4243461 | bytes 13205655 | solution.py:40
  535.4 8.9 %fusion.95 = f32[512,16,128]{2,1,0:T(8,128)} fusion(f32[8,512,16,128]{3,2,1,0:T(8,128)} %get-tuple-element.580, s32[]{:T(128)S(6)} %select_n.269, f32[512,16,128]{2,1,0:T(8,128)} %get-tuple-element.565, f32[512,16]{1,0:T(8,128)S(1)} %get-tuple-element.577, f32[512,16]{1,0:T(8,128)S(1)} %get-tuple-element.512, f32[512,16]{1,0:T(8,128)S(1)} %get-tuple-element.513), kind=kLoop, calls=%fused_computation.23.clone.1 | loop fusion | flops 4194304 | bytes 12681220 | tf_op jit(solution)/shard_map/while/body/eval_jaxpr/div | solution.py:91
  544.9 8.9 %fusion.95 = f32[512,16,128]{2,1,0:T(8,128)} fusion(f32[8,512,16,128]{3,2,1,0:T(8,128)} %get-tuple-element.580, s32[]{:T(128)S(6)} %select_n.269, f32[512,16,128]{2,1,0:T(8,128)} %get-tuple-element.565, f32[512,16]{1,0:T(8,128)S(1)} %get-tuple-element.577, f32[512,16]{1,0:T(8,128)S(1)} %get-tuple-element.512, f32[512,16]{1,0:T(8,128)S(1)} %get-tuple-element.513), kind=kLoop, calls=%fused_computation.23.clone.1 | loop fusion | flops 4194304 | bytes 12681220 | tf_op jit(solution)/shard_map/while/body/eval_jaxpr/div | solution.py:91
  554.3 8.9 %fusion.95 = f32[512,16,128]{2,1,0:T(8,128)} fusion(f32[8,512,16,128]{3,2,1,0:T(8,128)} %get-tuple-element.580, s32[]{:T(128)S(6)} %select_n.269, f32[512,16,128]{2,1,0:T(8,128)} %get-tuple-element.565, f32[512,16]{1,0:T(8,128)S(1)} %get-tuple-element.577, f32[512,16]{1,0:T(8,128)S(1)} %get-tuple-element.512, f32[512,16]{1,0:T(8,128)S(1)} %get-tuple-element.513), kind=kLoop, calls=%fused_computation.23.clone.1 | loop fusion | flops 4194304 | bytes 12681220 | tf_op jit(solution)/shard_map/while/body/eval_jaxpr/div | solution.py:91
  563.7 9.0 %fusion.95 = f32[512,16,128]{2,1,0:T(8,128)} fusion(f32[8,512,16,128]{3,2,1,0:T(8,128)} %get-tuple-element.580, s32[]{:T(128)S(6)} %select_n.269, f32[512,16,128]{2,1,0:T(8,128)} %get-tuple-element.565, f32[512,16]{1,0:T(8,128)S(1)} %get-tuple-element.577, f32[512,16]{1,0:T(8,128)S(1)} %get-tuple-element.512, f32[512,16]{1,0:T(8,128)S(1)} %get-tuple-element.513), kind=kLoop, calls=%fused_computation.23.clone.1 | loop fusion | flops 4194304 | bytes 12681220 | tf_op jit(solution)/shard_map/while/body/eval_jaxpr/div | solution.py:91
  573.2 9.0 %fusion.95 = f32[512,16,128]{2,1,0:T(8,128)} fusion(f32[8,512,16,128]{3,2,1,0:T(8,128)} %get-tuple-element.580, s32[]{:T(128)S(6)} %select_n.269, f32[512,16,128]{2,1,0:T(8,128)} %get-tuple-element.565, f32[512,16]{1,0:T(8,128)S(1)} %get-tuple-element.577, f32[512,16]{1,0:T(8,128)S(1)} %get-tuple-element.512, f32[512,16]{1,0:T(8,128)S(1)} %get-tuple-element.513), kind=kLoop, calls=%fused_computation.23.clone.1 | loop fusion | flops 4194304 | bytes 12681220 | tf_op jit(solution)/shard_map/while/body/eval_jaxpr/div | solution.py:91
  582.7 8.9 %fusion.95 = f32[512,16,128]{2,1,0:T(8,128)} fusion(f32[8,512,16,128]{3,2,1,0:T(8,128)} %get-tuple-element.580, s32[]{:T(128)S(6)} %select_n.269, f32[512,16,128]{2,1,0:T(8,128)} %get-tuple-element.565, f32[512,16]{1,0:T(8,128)S(1)} %get-tuple-element.577, f32[512,16]{1,0:T(8,128)S(1)} %get-tuple-element.512, f32[512,16]{1,0:T(8,128)S(1)} %get-tuple-element.513), kind=kLoop, calls=%fused_computation.23.clone.1 | loop fusion | flops 4194304 | bytes 12681220 | tf_op jit(solution)/shard_map/while/body/eval_jaxpr/div | solution.py:91
  592.1 8.9 %fusion.95 = f32[512,16,128]{2,1,0:T(8,128)} fusion(f32[8,512,16,128]{3,2,1,0:T(8,128)} %get-tuple-element.580, s32[]{:T(128)S(6)} %select_n.269, f32[512,16,128]{2,1,0:T(8,128)} %get-tuple-element.565, f32[512,16]{1,0:T(8,128)S(1)} %get-tuple-element.577, f32[512,16]{1,0:T(8,128)S(1)} %get-tuple-element.512, f32[512,16]{1,0:T(8,128)S(1)} %get-tuple-element.513), kind=kLoop, calls=%fused_computation.23.clone.1 | loop fusion | flops 4194304 | bytes 12681220 | tf_op jit(solution)/shard_map/while/body/eval_jaxpr/div | solution.py:91
  603.7 3.3 convolution_convert_fusion
  607.1 60.9 %reduce-scatter.2.cloned.1.call-done = bf16[32,2048]{1,0:T(8,128)(2,1)} async-done(((bf16[512,2048]{1,0:T(8,128)(2,1)}), bf16[32,2048]{1,0:T(8,128)(2,1)}) %reduce-scatter.2.cloned.1.call-update) | async-done | bytes 131088 | tf_op jit(solution)/shard_map/reduce_scatter | solution.py:190
  (155 shorter events, 53.7 us)
Async XLA Ops:
  6.5 129.8 %copy-start = (bf16[3,128,1,256]{3,1,2,0:T(8,128)(2,1)S(1)}, bf16[3,128,1,256]{3,1,2,0:T(8,128)(2,1)}, u32[]{:S(2)}) copy-start(bf16[3,128,1,256]{3,1,2,0:T(8,128)(2,1)} %param.26) | copy-start | bytes 589828
  6.5 94.4 %all-gather.9.cloned.1.call-start = ((), (), s32[]{:S(2)}) async-start(), calls=%async_computation.2 | async-start | bytes 3342336 | tf_op jit(solution)/shard_map/all_gather | solution.py:126
  7.3 124.0 %all-gather.7.cloned.1.call-start = ((), (), s32[]{:S(2)}) async-start(), calls=%async_computation.1 | async-start | bytes 4718592 | tf_op jit(solution)/shard_map/all_gather | solution.py:121
  10.6 170.7 %all-gather.15.cloned.1.call-start = ((), (), s32[]{:S(2)}) async-start(), calls=%async_computation.6 | async-start | bytes 2359296 | tf_op jit(solution)/shard_map/all_gather | solution.py:148
  11.9 12.8 %collective-permute-start = (bf16[256,3,1,256]{0,3,1,2:T(8,128)(2,1)S(1)}, bf16[256,3,1,256]{0,3,1,2:T(8,128)(2,1)S(1)}, u32[]{:S(2)}, u32[]{:S(2)}) collective-permute-start(bf16[256,3,1,256]{0,3,1,2:T(8,128)(2,1)S(1)} %copy.56), channel_id=1, source_target_pairs={{0,16},{16,32},{32,48},{48,64},{64,80},{80,96},{96,112},{112,128},... | collective-permute-start | bytes 1179656 | tf_op jit(solution)/shard_map/ppermute | solution.py:25
  14.0 10.6 %collective-permute-start.1 = (bf16[256,3,1,256]{0,3,1,2:T(8,128)(2,1)S(1)}, bf16[256,3,1,256]{0,3,1,2:T(8,128)(2,1)S(1)}, u32[]{:S(2)}, u32[]{:S(2)}) collective-permute-start(bf16[256,3,1,256]{0,3,1,2:T(8,128)(2,1)S(1)} %copy.56), channel_id=1, source_target_pairs={{0,240},{16,0},{32,16},{48,32},{64,48},{80,64},{96,80},{112,96},{1... | collective-permute-start | bytes 1179656 | tf_op jit(solution)/shard_map/ppermute | solution.py:28
  24.7 15.7 %copy-start.7 = (bf16[256,3,1,256]{0,3,1,2:T(8,128)(2,1)}, bf16[256,3,1,256]{0,3,1,2:T(8,128)(2,1)S(1)}, u32[]{:S(2)}) copy-start(bf16[256,3,1,256]{0,3,1,2:T(8,128)(2,1)S(1)} %collective-permute-done) | copy-start | bytes 1179652
  24.7 10.9 %collective-permute-start.2 = (bf16[256,3,1,256]{0,3,1,2:T(8,128)(2,1)S(1)}, bf16[256,3,1,256]{0,3,1,2:T(8,128)(2,1)S(1)}, u32[]{:S(2)}, u32[]{:S(2)}) collective-permute-start(bf16[256,3,1,256]{0,3,1,2:T(8,128)(2,1)S(1)} %collective-permute-done), channel_id=1, source_target_pairs={{0,16},{16,32},{32,48},{48,64},{64,80},{80,96},{96,112},{112,128},... | collective-permute-start | bytes 1179656 | tf_op jit(solution)/shard_map/ppermute | solution.py:25
  24.7 10.9 %collective-permute-start.3 = (bf16[256,3,1,256]{0,3,1,2:T(8,128)(2,1)S(1)}, bf16[256,3,1,256]{0,3,1,2:T(8,128)(2,1)S(1)}, u32[]{:S(2)}, u32[]{:S(2)}) collective-permute-start(bf16[256,3,1,256]{0,3,1,2:T(8,128)(2,1)S(1)} %collective-permute-done.1), channel_id=1, source_target_pairs={{0,240},{16,0},{32,16},{48,32},{64,48},{80,64},{96,80},{112,96},{1... | collective-permute-start | bytes 1179656 | tf_op jit(solution)/shard_map/ppermute | solution.py:28
  35.6 9.9 %collective-permute-start.4 = (bf16[256,3,1,256]{0,3,1,2:T(8,128)(2,1)S(1)}, bf16[256,3,1,256]{0,3,1,2:T(8,128)(2,1)S(1)}, u32[]{:S(2)}, u32[]{:S(2)}) collective-permute-start(bf16[256,3,1,256]{0,3,1,2:T(8,128)(2,1)S(1)} %collective-permute-done.2), channel_id=1, source_target_pairs={{0,16},{16,32},{32,48},{48,64},{64,80},{80,96},{96,112},{112,128},... | collective-permute-start | bytes 1179656 | tf_op jit(solution)/shard_map/ppermute | solution.py:25
  35.6 9.9 %collective-permute-start.5 = (bf16[256,3,1,256]{0,3,1,2:T(8,128)(2,1)S(1)}, bf16[256,3,1,256]{0,3,1,2:T(8,128)(2,1)S(1)}, u32[]{:S(2)}, u32[]{:S(2)}) collective-permute-start(bf16[256,3,1,256]{0,3,1,2:T(8,128)(2,1)S(1)} %collective-permute-done.3), channel_id=1, source_target_pairs={{0,240},{16,0},{32,16},{48,32},{64,48},{80,64},{96,80},{112,96},{1... | collective-permute-start | bytes 1179656 | tf_op jit(solution)/shard_map/ppermute | solution.py:28
  45.5 10.0 %copy-start.5 = (bf16[256,3,1,256]{0,3,1,2:T(8,128)(2,1)}, bf16[256,3,1,256]{0,3,1,2:T(8,128)(2,1)S(1)}, u32[]{:S(2)}) copy-start(bf16[256,3,1,256]{0,3,1,2:T(8,128)(2,1)S(1)} %collective-permute-done.4) | copy-start | bytes 1179652
  45.5 9.9 %collective-permute-start.6 = (bf16[256,3,1,256]{0,3,1,2:T(8,128)(2,1)S(1)}, bf16[256,3,1,256]{0,3,1,2:T(8,128)(2,1)S(1)}, u32[]{:S(2)}, u32[]{:S(2)}) collective-permute-start(bf16[256,3,1,256]{0,3,1,2:T(8,128)(2,1)S(1)} %collective-permute-done.4), channel_id=1, source_target_pairs={{0,16},{16,32},{32,48},{48,64},{64,80},{80,96},{96,112},{112,128},... | collective-permute-start | bytes 1179656 | tf_op jit(solution)/shard_map/ppermute | solution.py:25
  45.5 15.1 %collective-permute-start.7 = (bf16[256,3,1,256]{0,3,1,2:T(8,128)(2,1)S(1)}, bf16[256,3,1,256]{0,3,1,2:T(8,128)(2,1)S(1)}, u32[]{:S(2)}, u32[]{:S(2)}) collective-permute-start(bf16[256,3,1,256]{0,3,1,2:T(8,128)(2,1)S(1)} %collective-permute-done.5), channel_id=1, source_target_pairs={{0,240},{16,0},{32,16},{48,32},{64,48},{80,64},{96,80},{112,96},{1... | collective-permute-start | bytes 1179656 | tf_op jit(solution)/shard_map/ppermute | solution.py:28
  55.5 10.7 %collective-permute-start.8 = (bf16[256,3,1,256]{0,3,1,2:T(8,128)(2,1)S(1)}, bf16[256,3,1,256]{0,3,1,2:T(8,128)(2,1)S(1)}, u32[]{:S(2)}, u32[]{:S(2)}) collective-permute-start(bf16[256,3,1,256]{0,3,1,2:T(8,128)(2,1)S(1)} %collective-permute-done.6), channel_id=1, source_target_pairs={{0,16},{16,32},{32,48},{48,64},{64,80},{80,96},{96,112},{112,128},... | collective-permute-start | bytes 1179656 | tf_op jit(solution)/shard_map/ppermute | solution.py:25
  55.5 4.3 copy-start.8
  55.5 12.4 %copy-start.6 = (bf16[256,3,1,256]{0,3,1,2:T(8,128)(2,1)S(1)}, bf16[256,3,1,256]{0,3,1,2:T(8,128)(2,1)}, u32[]{:S(2)}) copy-start(bf16[256,3,1,256]{0,3,1,2:T(8,128)(2,1)} %copy-done.5) | copy-start | bytes 1179652
  60.6 9.5 %collective-permute-start.9 = (bf16[256,3,1,256]{0,3,1,2:T(8,128)(2,1)S(1)}, bf16[256,3,1,256]{0,3,1,2:T(8,128)(2,1)S(1)}, u32[]{:S(2)}, u32[]{:S(2)}) collective-permute-start(bf16[256,3,1,256]{0,3,1,2:T(8,128)(2,1)S(1)} %collective-permute-done.7), channel_id=1, source_target_pairs={{0,240},{16,0},{32,16},{48,32},{64,48},{80,64},{96,80},{112,96},{1... | collective-permute-start | bytes 1179656 | tf_op jit(solution)/shard_map/ppermute | solution.py:28
  66.2 10.1 %collective-permute-start.10 = (bf16[256,3,1,256]{0,3,1,2:T(8,128)(2,1)S(1)}, bf16[256,3,1,256]{0,3,1,2:T(8,128)(2,1)S(1)}, u32[]{:S(2)}, u32[]{:S(2)}) collective-permute-start(bf16[256,3,1,256]{0,3,1,2:T(8,128)(2,1)S(1)} %collective-permute-done.8), channel_id=1, source_target_pairs={{0,16},{16,32},{32,48},{48,64},{64,80},{80,96},{96,112},{112,128},... | collective-permute-start | bytes 1179656 | tf_op jit(solution)/shard_map/ppermute | solution.py:25
  70.1 11.2 %collective-permute-start.11 = (bf16[256,3,1,256]{0,3,1,2:T(8,128)(2,1)S(1)}, bf16[256,3,1,256]{0,3,1,2:T(8,128)(2,1)S(1)}, u32[]{:S(2)}, u32[]{:S(2)}) collective-permute-start(bf16[256,3,1,256]{0,3,1,2:T(8,128)(2,1)S(1)} %collective-permute-done.9), channel_id=1, source_target_pairs={{0,240},{16,0},{32,16},{48,32},{64,48},{80,64},{96,80},{112,96},{1... | collective-permute-start | bytes 1179656 | tf_op jit(solution)/shard_map/ppermute | solution.py:28
  76.3 11.3 %collective-permute-start.12 = (bf16[256,3,1,256]{0,3,1,2:T(8,128)(2,1)S(1)}, bf16[256,3,1,256]{0,3,1,2:T(8,128)(2,1)S(1)}, u32[]{:S(2)}, u32[]{:S(2)}) collective-permute-start(bf16[256,3,1,256]{0,3,1,2:T(8,128)(2,1)S(1)} %collective-permute-done.10), channel_id=1, source_target_pairs={{0,16},{16,32},{32,48},{48,64},{64,80},{80,96},{96,112},{112,128},... | collective-permute-start | bytes 1179656 | tf_op jit(solution)/shard_map/ppermute | solution.py:25
  81.3 12.3 %collective-permute-start.13 = (bf16[256,3,1,256]{0,3,1,2:T(8,128)(2,1)S(1)}, bf16[256,3,1,256]{0,3,1,2:T(8,128)(2,1)S(1)}, u32[]{:S(2)}, u32[]{:S(2)}) collective-permute-start(bf16[256,3,1,256]{0,3,1,2:T(8,128)(2,1)S(1)} %collective-permute-done.11), channel_id=1, source_target_pairs={{0,240},{16,0},{32,16},{48,32},{64,48},{80,64},{96,80},{112,96},{1... | collective-permute-start | bytes 1179656 | tf_op jit(solution)/shard_map/ppermute | solution.py:28
  87.6 12.5 %collective-permute-start.14 = (bf16[256,3,1,256]{0,3,1,2:T(8,128)(2,1)S(1)}, bf16[256,3,1,256]{0,3,1,2:T(8,128)(2,1)S(1)}, u32[]{:S(2)}, u32[]{:S(2)}) collective-permute-start(bf16[256,3,1,256]{0,3,1,2:T(8,128)(2,1)S(1)} %collective-permute-done.12), channel_id=1, source_target_pairs={{0,16},{16,32},{32,48},{48,64},{64,80},{80,96},{96,112},{112,128},... | collective-permute-start | bytes 1179656 | tf_op jit(solution)/shard_map/ppermute | solution.py:25
  131.2 5.6 copy-start.12
  144.0 386.5 %all-gather.11.cloned.1.call-start = ((), (), s32[]{:S(2)}) async-start(), calls=%async_computation.3 | async-start | bytes 37748736 | tf_op jit(solution)/shard_map/all_gather | solution.py:34
  154.4 7.9 %copy-start.10 = (s32[1,16]{1,0:T(1,128)S(1)}, s32[1,16]{1,0:T(1,128)}, u32[]{:S(2)}) copy-start(s32[1,16]{1,0:T(1,128)} %param.34) | copy-start | bytes 196
  154.5 8.6 %copy-start.11 = (s32[8,128]{1,0:T(8,128)S(1)}, s32[8,128]{1,0:T(8,128)}, u32[]{:S(2)}) copy-start(s32[8,128]{1,0:T(8,128)} %constant.310.clone.1) | copy-start | bytes 12292
  173.3 5.1 copy-start.2
  227.0 6.3 copy-start.3
  227.0 6.3 copy-start.4
  232.5 1.9 copy-start.9
  232.6 371.1 %all-gather.13.cloned.1.call-start = ((), (), s32[]{:S(2)}) async-start(), calls=%async_computation.4 | async-start | bytes 1114112 | tf_op jit(solution)/shard_map/all_gather | solution.py:189
  233.2 434.8 %reduce-scatter.2.cloned.1.call-start = ((), (), s32[]{:S(2)}) async-start(), calls=%async_computation.5 | async-start | bytes 2228224 | tf_op jit(solution)/shard_map/reduce_scatter | solution.py:190
  603.3 3.7 copy-start.13
  603.3 66.3 %copy-start.1 = (bf16[3,128,1,256]{3,1,2,0:T(8,128)(2,1)S(1)}, bf16[3,128,1,256]{3,1,2,0:T(8,128)(2,1)}, u32[]{:S(2)}) copy-start(bf16[3,128,1,256]{3,1,2,0:T(8,128)(2,1)} %param.26) | copy-start | bytes 589828
Sparse Core Ops, SparseCore 0:
  9.1 67.9 all-gather.8
  79.0 52.1 all-gather.6
  144.1 34.2 all-gather.14
  232.7 297.6 all-gather.10
  532.7 45.5 all-gather.12
  607.1 60.7 reduce-scatter.1
